TPU v7x, 32 devices: a whole 2x2x4 slice. The times are simulated.
32 devices in a mesh: shard: 2 (over y), ctx: 4 (over z), tp: 4 (over x, core).
Axes of the slice: x: 2, y: 2, z: 4, core: 2. Of those that a mesh axis runs over, the one named last changes fastest.
Arguments:
- inputs: bfloat16 [2, 4096, 768], P('shard', 'ctx'), may hold values from -6 to 6
- lengths: int32 [2], P('shard'), may hold values from 1024 to 4096, as said below
- global_blocks: int32 [2, 2], P('shard'), may hold values from 0 to 15, as said below
- random_blocks: int32 [2, 64, 3], P('shard', 'ctx'), may hold values from 0 to 63
- master_blocks: float32 [768, 96, 96], P(('shard', 'ctx', 'tp'))
- outer_vectors: float32 [6, 768], replicated
- inner_biases: float32 [4, 1152], P('tp'), may hold values from -4 to 4
- left_stats: float32 [768, 96, 96], P(('shard', 'ctx', 'tp')), as said below
- right_stats: float32 [768, 96, 96], P(('shard', 'ctx', 'tp')), as said below
- left_roots: float32 [768, 96, 96], P(('shard', 'ctx', 'tp')), as said below
- right_roots: float32 [768, 96, 96], P(('shard', 'ctx', 'tp')), as said below
- cotangent: bfloat16 [2, 4096, 768], P('shard', 'ctx'), may hold values from -6 to 6
Outputs:
- output: bfloat16 [2, 4096, 768], P('shard', 'ctx')
- input_grad: bfloat16 [2, 4096, 768], P('shard', 'ctx')
- block_grads: float32 [768, 96, 96], P(('shard', 'ctx', 'tp'))
- outer_grads: float32 [6, 768], P(None, ('shard', 'ctx'))
- inner_grads: float32 [4, 1152], P('tp', ('shard', 'ctx'))
- maxima: float32 [12], P('tp')
- left_new: float32 [768, 96, 96], P(('shard', 'ctx', 'tp'))
- right_new: float32 [768, 96, 96], P(('shard', 'ctx', 'tp'))
- new_blocks: float32 [768, 96, 96], P(('shard', 'ctx', 'tp'))
- new_outer: float32 [6, 768], P(None, ('shard', 'ctx'))
- new_inner: float32 [4, 1152], P('tp', ('shard', 'ctx'))
Inputs may be any that keep to these rules, and one draw needn't show every extreme that they name: `lengths`: sequence 0 holds 4096 valid tokens. `global_blocks`: the two ids of a sequence differ. `left_stats`: each block is symmetric. `right_stats`: each block is symmetric. `left_roots`: each block is symmetric. `right_roots`: each block is symmetric.
All inputs are finite; a program needn't handle non-finite values.
Results may differ from a plain program's by a relative error of at most 0.018.
Values may be sent and summed in bfloat16 or wider, within the bound.
No kernel may reach another device: no remote copies, remote signals or barrier semaphores. Data moves between devices by JAX's collectives and lax.ppermute only.
A program may use at most 192 MiB of HBM per device.

v0:
```python
import jax
import jax.numpy as jnp
from jax import lax
from jax.sharding import PartitionSpec as P

D = 768
HEADS = 12
HEAD = 64
FF = 3072
BLOCK = 64
SEQ = 4096
PB = 96
eps_norm = 1e-06
tau_clip = 9.0
rate_matrix = 0.3
rate_vector = 0.001
neg_large = -1e30
high = lax.Precision.HIGHEST


def layer_norm(values, gain, shift):
    mean_val = jnp.mean(values, axis=-1, keepdims=True)
    centred = values - mean_val
    var_val = jnp.mean(centred * centred, axis=-1, keepdims=True)
    return centred * lax.rsqrt(var_val + eps_norm) * gain + shift


def gelu_tanh(values):
    return jax.nn.gelu(values, approximate=True)


def to_grid(blocks, row_count, col_count):
    shaped = blocks.reshape(row_count // PB, col_count // PB, PB, PB)
    return shaped.transpose(0, 2, 1, 3).reshape(row_count, col_count)


def from_grid(matrix):
    row_count, col_count = matrix.shape
    shaped = matrix.reshape(row_count // PB, PB, col_count // PB, PB)
    return shaped.transpose(0, 2, 1, 3).reshape(-1, PB, PB)


def unpack_weights(whole, head_cols, unit_count):
    first_end = D // PB * (3 * head_cols // PB)
    second_end = first_end + head_cols // PB * (D // PB)
    third_end = second_end + D // PB * (unit_count // PB)
    return (
        to_grid(whole[:first_end], D, 3 * head_cols),
        to_grid(whole[first_end:second_end], head_cols, D),
        to_grid(whole[second_end:third_end], D, unit_count),
        to_grid(whole[third_end:], unit_count, D),
    )


def block_layout(slot_length, global_ids, random_ids, first_block, rows_blocks, block_count):
    rows = first_block + jnp.arange(rows_blocks, dtype=jnp.int32)
    window = jnp.stack([rows - 1, rows, rows + 1], axis=1)
    globals_row = jnp.broadcast_to(global_ids[None, :], (rows_blocks, 2))
    listed = jnp.concatenate([window, globals_row, random_ids], axis=1)
    inside = (listed >= 0) & (listed < block_count)
    clipped = jnp.clip(listed, 0, block_count - 1)
    key_pos = listed[:, :, None] * BLOCK + jnp.arange(BLOCK, dtype=jnp.int32)[None, None, :]
    key_mask = (inside[:, :, None] & (key_pos < slot_length)).reshape(rows_blocks, -1)
    query_pos = (first_block * BLOCK + jnp.arange(rows_blocks * BLOCK, dtype=jnp.int32)).reshape(
        rows_blocks, BLOCK
    )
    return (clipped, key_mask, query_pos < slot_length)


def pick_blocks(full_rows, clipped, head_count):
    block_count = full_rows.shape[0] // BLOCK
    picked = full_rows.reshape(block_count, BLOCK, -1)[clipped]
    return picked.reshape(clipped.shape[0], clipped.shape[1] * BLOCK, head_count, HEAD)


def attend_scores(query_blocks, key_blocks):
    return jnp.einsum(
        "lqhd,lkhd->lhqk", query_blocks, key_blocks, preferred_element_type=jnp.float32
    ) * HEAD ** (-0.5)


def probs_again(query_blocks, d_out_blocks, key_blocks, value_blocks, key_mask, lse_blk):
    raw_scores = attend_scores(query_blocks, key_blocks)
    probs = jnp.exp(jnp.where(key_mask[:, None, None, :], raw_scores, neg_large) - lse_blk)
    d_probs = jnp.einsum(
        "lqhd,lkhd->lhqk", d_out_blocks, value_blocks, preferred_element_type=jnp.float32
    )
    return (probs, d_probs)


def group_back(
    query_blocks,
    d_out_blocks,
    key_src,
    value_src,
    clipped,
    key_mask,
    lse_blk,
    delta_blk,
    block_count,
):
    rows_blocks, _, heads_here, _ = query_blocks.shape
    head_cols = heads_here * HEAD
    key_blocks = pick_blocks(key_src, clipped, heads_here)
    value_blocks = pick_blocks(value_src, clipped, heads_here)
    probs, d_probs = probs_again(
        query_blocks, d_out_blocks, key_blocks, value_blocks, key_mask, lse_blk
    )
    delta_blk = jnp.sum(probs * d_probs, axis=-1, keepdims=True)
    d_scores = (probs * (d_probs - delta_blk)).astype(jnp.bfloat16)
    d_query = jnp.einsum(
        "lhqk,lkhd->lqhd", d_scores, key_blocks, preferred_element_type=jnp.float32
    ) * HEAD ** (-0.5)
    d_key_blocks = jnp.einsum(
        "lhqk,lqhd->lkhd", d_scores, query_blocks, preferred_element_type=jnp.float32
    ) * HEAD ** (-0.5)
    d_value_blocks = jnp.einsum(
        "lhqk,lqhd->lkhd",
        probs.astype(jnp.bfloat16),
        d_out_blocks,
        preferred_element_type=jnp.float32,
    )
    listed_count = clipped.shape[1]
    d_key_full = (
        jnp.zeros((block_count, BLOCK, head_cols), jnp.float32)
        .at[clipped]
        .add(d_key_blocks.reshape(rows_blocks, listed_count, BLOCK, head_cols))
    )
    d_value_full = (
        jnp.zeros((block_count, BLOCK, head_cols), jnp.float32)
        .at[clipped]
        .add(d_value_blocks.reshape(rows_blocks, listed_count, BLOCK, head_cols))
    )
    return (
        d_query.reshape(-1, head_cols),
        d_key_full.reshape(-1, head_cols),
        d_value_full.reshape(-1, head_cols),
    )


def per_device(
    inputs,
    lengths,
    global_blocks,
    random_blocks,
    master_blocks,
    outer_vectors,
    inner_biases,
    left_stats,
    right_stats,
    left_roots,
    right_roots,
    cotangent,
):
    tensor_count = lax.axis_size("tp")
    owner_count = lax.axis_size(("shard", "ctx"))
    heads_here = HEADS // tensor_count
    head_cols = heads_here * HEAD
    unit_count = FF // tensor_count
    slot_count, ctx_tokens, _ = inputs.shape
    rows_blocks = ctx_tokens // BLOCK
    block_count = SEQ // BLOCK
    ctx_index = lax.axis_index("ctx")
    owner_index = lax.axis_index(("shard", "ctx"))
    gathered = lax.all_gather(
        master_blocks.astype(jnp.bfloat16), ("shard", "ctx"), axis=0, tiled=True
    )
    w_qkv, w_out, w_up, w_down = unpack_weights(gathered, head_cols, unit_count)
    flat_in = inputs.reshape(-1, D)
    inner_row = inner_biases[0]
    q_bias = inner_row[:head_cols]
    v_bias = inner_row[head_cols : 2 * head_cols]
    up_bias = inner_row[2 * head_cols :]
    projected = jnp.dot(flat_in, w_qkv, preferred_element_type=jnp.float32)
    queries = (projected[:, :head_cols] + q_bias).astype(jnp.bfloat16)
    key_rows = (
        projected[:, head_cols : 2 * head_cols]
        .astype(jnp.bfloat16)
        .reshape(slot_count, ctx_tokens, head_cols)
    )
    value_rows = (
        (projected[:, 2 * head_cols :] + v_bias)
        .astype(jnp.bfloat16)
        .reshape(slot_count, ctx_tokens, head_cols)
    )
    keys_all, values_all = (
        lax.all_gather(key_rows, "ctx", axis=1, tiled=True),
        lax.all_gather(value_rows, "ctx", axis=1, tiled=True),
    )
    query_slots = queries.reshape(slot_count, ctx_tokens, head_cols)
    peak_logit = jnp.full((heads_here,), neg_large, jnp.float32)
    slot_index = 0
    clipped, key_mask, query_mask = block_layout(
        lengths[slot_index],
        global_blocks[slot_index],
        random_blocks[slot_index],
        ctx_index * rows_blocks,
        rows_blocks,
        block_count,
    )
    layouts = [(clipped, key_mask)]
    query_blocks = query_slots[slot_index].reshape(rows_blocks, BLOCK, heads_here, HEAD)
    key_blocks = pick_blocks(keys_all[slot_index], clipped, heads_here)
    value_blocks = pick_blocks(values_all[slot_index], clipped, heads_here)
    raw_scores = attend_scores(query_blocks, key_blocks)
    both_mask = key_mask[:, None, None, :] & query_mask[:, None, :, None]
    peak_logit = jnp.maximum(
        peak_logit, jnp.max(jnp.where(both_mask, raw_scores, neg_large), axis=(0, 2, 3))
    )
    masked = jnp.where(key_mask[:, None, None, :], raw_scores, neg_large)
    row_top = jnp.max(masked, axis=-1, keepdims=True)
    shifted = jnp.exp(masked - row_top)
    row_total = jnp.sum(shifted, axis=-1, keepdims=True)
    probs = shifted / row_total
    lse_list = [row_top + jnp.log(row_total)]
    attended = jnp.einsum(
        "lhqk,lkhd->lqhd",
        probs.astype(jnp.bfloat16),
        value_blocks,
        preferred_element_type=jnp.float32,
    )
    attended_list = attended.reshape(ctx_tokens, head_cols)
    attended_low = attended_list.astype(jnp.bfloat16)
    branch = (
        lax.psum(jnp.dot(attended_low, w_out, preferred_element_type=jnp.float32), "tp")
        + outer_vectors[0]
    )
    hidden_in = flat_in.astype(jnp.float32) + branch
    x_first = layer_norm(hidden_in, outer_vectors[2], outer_vectors[3])
    x_first_low = x_first.astype(jnp.bfloat16)
    gate_pre = jnp.dot(x_first_low, w_up, preferred_element_type=jnp.float32) + up_bias
    act_low = gelu_tanh(gate_pre).astype(jnp.bfloat16)
    ff_out = (
        lax.psum(jnp.dot(act_low, w_down, preferred_element_type=jnp.float32), "tp")
        + outer_vectors[1]
    )
    mixed_sum = x_first + ff_out
    result = layer_norm(mixed_sum, outer_vectors[4], outer_vectors[5])
    maxima = lax.pmax(peak_logit, ("shard", "ctx"))
    positions = ctx_index * ctx_tokens + jnp.arange(ctx_tokens, dtype=jnp.int32)
    row_valid = (positions[None, :] < lengths[:, None]).astype(jnp.float32).reshape(-1)
    d_result = cotangent.reshape(-1, D).astype(jnp.float32) * row_valid[:, None]
    regathered = lax.all_gather(
        master_blocks.astype(jnp.bfloat16), ("shard", "ctx"), axis=0, tiled=True
    )
    wb_qkv, wb_out, wb_up, wb_down = unpack_weights(regathered, head_cols, unit_count)
    _, back_second = jax.vjp(layer_norm, mixed_sum, outer_vectors[4], outer_vectors[5])
    d_mixed, d_gain2, d_shift2 = back_second(d_result)
    d_ff_low = d_mixed.astype(jnp.bfloat16)
    d_bias2 = jnp.sum(d_ff_low.astype(jnp.float32), axis=0)
    g_down = jnp.dot(act_low.T, d_ff_low, preferred_element_type=jnp.float32)
    d_act = jnp.dot(d_ff_low, wb_down.T, preferred_element_type=jnp.float32)
    _, back_gelu = jax.vjp(gelu_tanh, gate_pre)
    d_gate_low = back_gelu(d_act)[0].astype(jnp.bfloat16)
    d_upbias = jnp.sum(d_gate_low.astype(jnp.float32), axis=0)
    g_up = jnp.dot(x_first_low.T, d_gate_low, preferred_element_type=jnp.float32)
    d_first = d_mixed + lax.psum(
        jnp.dot(d_gate_low, wb_up.T, preferred_element_type=jnp.float32), "tp"
    )
    _, back_first = jax.vjp(layer_norm, hidden_in, outer_vectors[2], outer_vectors[3])
    d_hidden, d_gain1, d_shift1 = back_first(d_first)
    d_branch_low = d_hidden.astype(jnp.bfloat16)
    d_bias_out = jnp.sum(d_branch_low.astype(jnp.float32), axis=0)
    g_out = jnp.dot(attended_low.T, d_branch_low, preferred_element_type=jnp.float32)
    d_att_low = jnp.dot(d_branch_low, wb_out.T, preferred_element_type=jnp.float32).astype(
        jnp.bfloat16
    )
    d_att_slots = d_att_low.reshape(slot_count, ctx_tokens, head_cols)
    keys_back, values_back = (keys_all, values_all)
    slot_index = 0
    clipped, key_mask = layouts[slot_index]
    query_blocks = query_slots[slot_index].reshape(rows_blocks, BLOCK, heads_here, HEAD)
    d_out_blocks = d_att_slots[slot_index].reshape(rows_blocks, BLOCK, heads_here, HEAD)
    d_query, d_key_full, d_value_full = group_back(
        query_blocks,
        d_out_blocks,
        keys_back[slot_index],
        values_back[slot_index],
        clipped,
        key_mask,
        lse_list[slot_index],
        None,
        block_count,
    )
    dk_list = [d_key_full]
    dv_list = [d_value_full]
    d_keys, d_values = (
        lax.psum_scatter(
            jnp.stack(dk_list).astype(jnp.bfloat16), "ctx", scatter_dimension=1, tiled=True
        ).astype(jnp.float32),
        lax.psum_scatter(
            jnp.stack(dv_list).astype(jnp.bfloat16), "ctx", scatter_dimension=1, tiled=True
        ).astype(jnp.float32),
    )
    d_q_low = d_query.astype(jnp.bfloat16)
    d_k_low = d_keys.reshape(-1, head_cols).astype(jnp.bfloat16)
    d_v_low = d_values.reshape(-1, head_cols).astype(jnp.bfloat16)
    d_proj = jnp.concatenate([d_q_low, d_k_low, d_v_low], axis=1)
    d_qbias = jnp.sum(d_q_low.astype(jnp.float32), axis=0)
    d_vbias = jnp.sum(d_v_low.astype(jnp.float32), axis=0)
    g_qkv = jnp.dot(flat_in.T, d_proj, preferred_element_type=jnp.float32)
    d_inputs = d_hidden + lax.psum(
        jnp.dot(d_proj, wb_qkv.T, preferred_element_type=jnp.float32).astype(jnp.bfloat16), "tp"
    ).astype(jnp.float32)
    input_grad = d_inputs.reshape(inputs.shape).astype(jnp.bfloat16)
    blocks_grad = jnp.concatenate(
        [from_grid(g_qkv), from_grid(g_out), from_grid(g_up), from_grid(g_down)], axis=0
    )
    outer_part = jnp.stack([d_bias_out, d_bias2, d_gain1, d_shift1, d_gain2, d_shift2], axis=0)
    inner_part = jnp.concatenate([d_qbias, d_vbias, d_upbias])[None, :]
    block_sum, outer_sum, inner_sum = (
        lax.psum_scatter(blocks_grad, ("shard", "ctx"), scatter_dimension=0, tiled=True),
        lax.psum_scatter(outer_part, ("shard", "ctx"), scatter_dimension=1, tiled=True),
        lax.psum_scatter(inner_part, ("shard", "ctx"), scatter_dimension=1, tiled=True),
    )
    left_new = 0.5 * left_stats + 0.5 * jnp.einsum(
        "bij,bkj->bik", block_sum, block_sum, precision=high
    )
    right_new = 0.5 * right_stats + 0.5 * jnp.einsum(
        "bji,bjk->bik", block_sum, block_sum, precision=high
    )
    left_applied = jnp.einsum("bij,bjk->bik", left_roots, block_sum, precision=high)
    step_val = jnp.einsum("bij,bjk->bik", left_applied, right_roots, precision=high)
    clip_sqrt = jnp.sqrt(tau_clip / jnp.maximum(maxima, tau_clip))
    head_factor = jnp.repeat(clip_sqrt, HEAD)
    table = jnp.concatenate([head_factor, head_factor, jnp.ones((head_cols,), jnp.float32)])
    qkv_factor = jnp.tile(table.reshape(1, -1, PB), (D // PB, 1, 1)).reshape(-1, PB)
    blocks_here = master_blocks.shape[0]
    all_factor = jnp.concatenate(
        [qkv_factor, jnp.ones((blocks_here * owner_count - qkv_factor.shape[0], PB), jnp.float32)],
        axis=0,
    )
    own_factor = lax.dynamic_slice_in_dim(all_factor, owner_index * blocks_here, blocks_here, 0)
    new_blocks = (master_blocks - rate_matrix * step_val) * own_factor[:, None, :]
    outer_cols = D // owner_count
    own_outer = lax.dynamic_slice_in_dim(outer_vectors, owner_index * outer_cols, outer_cols, 1)
    new_outer = own_outer - rate_vector * outer_sum
    inner_cols = inner_biases.shape[1] // owner_count
    inner_factor = jnp.concatenate([head_factor, jnp.ones((head_cols + unit_count,), jnp.float32)])
    own_inner_factor = lax.dynamic_slice_in_dim(
        inner_factor, owner_index * inner_cols, inner_cols, 0
    )
    own_inner = lax.dynamic_slice_in_dim(inner_biases, owner_index * inner_cols, inner_cols, 1)
    new_inner = (own_inner - rate_vector * inner_sum) * own_inner_factor[None, :]
    output = result.reshape(inputs.shape).astype(jnp.bfloat16)
    return (
        output,
        input_grad,
        block_sum,
        outer_sum,
        inner_sum,
        maxima,
        left_new,
        right_new,
        new_blocks,
        new_outer,
        new_inner,
    )


def solution(mesh):
    return jax.shard_map(
        per_device,
        mesh=mesh,
        in_specs=(
            P("shard", "ctx", None),
            P("shard"),
            P("shard", None),
            P("shard", "ctx", None),
            P(("shard", "ctx", "tp"), None, None),
            P(),
            P("tp", None),
            P(("shard", "ctx", "tp"), None, None),
            P(("shard", "ctx", "tp"), None, None),
            P(("shard", "ctx", "tp"), None, None),
            P(("shard", "ctx", "tp"), None, None),
            P("shard", "ctx", None),
        ),
        out_specs=(
            P("shard", "ctx", None),
            P("shard", "ctx", None),
            P(("shard", "ctx", "tp"), None, None),
            P(None, ("shard", "ctx")),
            P("tp", ("shard", "ctx")),
            P("tp"),
            P(("shard", "ctx", "tp"), None, None),
            P(("shard", "ctx", "tp"), None, None),
            P(("shard", "ctx", "tp"), None, None),
            P(None, ("shard", "ctx")),
            P("tp", ("shard", "ctx")),
        ),
        check_vma=False,
    )
```

profile of v0, /device:TPU:0, one launch (start us, length us, event | category | flops | bytes accessed | tf_op | source)
XLA Modules:
  0.0 1027.7 jit_solution(3224889106006550222)
XLA Ops:
  9.6 83.2 %all-gather.6.cloned.1.call-done = bf16[192,96,96]{2,1,0:T(8,128)(2,1)} async-done(((bf16[24,96,96]{2,1,0:T(8,128)(2,1)}), bf16[192,96,96]{2,1,0:T(8,128)(2,1)}) %all-gather.6.cloned.1.call-update) | async-done | bytes 3538960 | tf_op jit(solution)/shard_map/all_gather | solution.py:165
  95.8 2.8 fusion.29
  109.1 27.4 %all-gather.10.cloned.1.call-done = bf16[4096,192]{0,1:T(8,128)(2,1)} async-done(((bf16[1024,192]{0,1:T(8,128)(2,1)}), bf16[4096,192]{0,1:T(8,128)(2,1)}) %all-gather.10.cloned.1.call-update) | async-done | bytes 1572880 | tf_op jit(solution)/shard_map/all_gather | solution.py:187
  136.5 3.1 copy.103
  139.7 2.7 gather_fusion.1
  142.4 15.9 %reshape.559 = bf16[16,512,3,64]{3,2,1,0:T(4,128)(2,1)} reshape(bf16[128,64,192]{2,1,0:T(8,128)(2,1)} %gather_fusion.1) | data formatting | bytes 6291456 | tf_op jit(solution)/shard_map/reshape | solution.py:73
  158.4 12.2 %copy.106 = bf16[16,512,3,64]{1,3,2,0:T(8,128)(2,1)} copy(bf16[16,512,3,64]{3,2,1,0:T(4,128)(2,1)} %reshape.559) | data formatting | bytes 6291456 | tf_op jit(solution)/shard_map/reshape | solution.py:73
  170.6 4.1 all-gather.8.cloned.1.call-done
  174.6 3.1 copy.98
  177.8 2.7 gather_fusion
  180.5 15.9 %reshape.558 = bf16[16,512,3,64]{3,2,1,0:T(4,128)(2,1)} reshape(bf16[128,64,192]{2,1,0:T(8,128)(2,1)} %gather_fusion) | data formatting | bytes 6291456 | tf_op jit(solution)/shard_map/reshape | solution.py:73
  196.4 12.3 %copy.107 = bf16[16,512,3,64]{1,3,2,0:T(8,128)(2,1)} copy(bf16[16,512,3,64]{3,2,1,0:T(4,128)(2,1)} %reshape.558) | data formatting | bytes 6291456 | tf_op jit(solution)/shard_map/reshape | solution.py:73
  208.7 3.2 fusion.24
  212.0 3.6 select_reduce_fusion
  216.2 2.7 fusion.39
  227.7 3.8 reshape.488
  233.3 3.9 reshape.490
  237.2 52.6 %all-reduce.7.cloned.1.call-done = f32[1024,768]{1,0:T(8,128)} async-done(((f32[1024,768]{1,0:T(8,128)}), f32[1024,768]{1,0:T(8,128)}) %all-reduce.7.cloned.1.call-update) | async-done | bytes 3145744 | tf_op jit(solution)/shard_map/psum | solution.py:225
  289.8 2.4 fusion.64
  297.7 3.8 fusion.59
  302.4 67.8 %all-reduce.9.cloned.1.call-done = f32[1024,768]{1,0:T(8,128)} async-done(((f32[1024,768]{1,0:T(8,128)}), f32[1024,768]{1,0:T(8,128)}) %all-reduce.9.cloned.1.call-update) | async-done | bytes 3145744 | tf_op jit(solution)/shard_map/psum | solution.py:234
  370.2 3.9 fusion.63
  377.8 2.8 fusion.62
  381.5 2.6 copy-done.76
  384.2 4.3 convert_reduce_fusion
  389.6 3.1 fusion.69
  393.6 67.9 %all-reduce.11.cloned.1.call-done = f32[1024,768]{1,0:T(8,128)} async-done(((f32[1024,768]{1,0:T(8,128)}), f32[1024,768]{1,0:T(8,128)}) %all-reduce.11.cloned.1.call-update) | async-done | bytes 3145744 | tf_op jit(solution)/shard_map/psum | solution.py:257
  461.5 5.4 multiply_reduce_fusion.1
  473.4 7.2 fusion.20
  480.6 15.1 %copy.136 = f32[16,512,3,64]{3,2,1,0:T(4,128)} copy(f32[16,512,3,64]{1,3,2,0:T(8,128)} %fusion.20) | data formatting | bytes 12582912 | tf_op jit(solution)/shard_map/reshape | solution.py:132
  495.7 18.9 %reshape.553 = f32[128,64,192]{2,1,0:T(8,128)} reshape(f32[16,512,3,64]{3,2,1,0:T(4,128)} %copy.136) | data formatting | bytes 12582912 | tf_op jit(solution)/shard_map/reshape | solution.py:132
  514.6 2.5 broadcast.358.clone
  517.0 26.2 %scatter_fusion.1 = f32[64,64,192]{2,1,0:T(8,128)} fusion(f32[64,64,192]{2,1,0:T(8,128)} %broadcast.358.clone, s32[128]{0:T(128)S(1)} %reshape.508, f32[128,64,192]{2,1,0:T(8,128)} %reshape.553), kind=kCustom, calls=%fused_computation.3 | custom fusion | flops 1572864 | bytes 18874880 | tf_op jit(solution)/shard_map/scatter-add | solution.py:132
  543.2 2.5 convert_element_type.178
  545.7 2.7 copy.123
  548.7 6.7 multiply_reduce_fusion
  555.4 3.9 multiply_convert_fusion
  560.9 3.6 multiply_bitcast_fusion
  564.5 15.1 %copy.135 = f32[16,512,3,64]{3,2,1,0:T(4,128)} copy(f32[16,512,3,64]{1,3,2,0:T(8,128)} %multiply_bitcast_fusion) | data formatting | bytes 12582912 | tf_op jit(solution)/shard_map/reshape | solution.py:127
  579.6 18.9 %reshape.552 = f32[128,64,192]{2,1,0:T(8,128)} reshape(f32[16,512,3,64]{3,2,1,0:T(4,128)} %copy.135) | data formatting | bytes 12582912 | tf_op jit(solution)/shard_map/reshape | solution.py:127
  598.5 2.5 broadcast.358.clone.1
  601.0 26.2 %scatter_fusion = f32[64,64,192]{2,1,0:T(8,128)} fusion(f32[64,64,192]{2,1,0:T(8,128)} %broadcast.358.clone.1, s32[128]{0:T(128)S(1)} %reshape.508, f32[128,64,192]{2,1,0:T(8,128)} %reshape.552), kind=kCustom, calls=%fused_computation.2 | custom fusion | flops 1572864 | bytes 18874880 | tf_op jit(solution)/shard_map/scatter-add | solution.py:127
  627.1 2.5 convert_element_type.174
  629.6 2.8 copy.119
  632.7 4.3 fusion.58
  637.0 2.6 reshape.498
  639.5 4.3 copy.127
  645.3 2.6 reshape.496
  647.8 4.3 copy.126
  664.6 3.4 reduce-scatter.10.cloned.1.call-done
  668.0 4.1 convolution_convert_fusion
  674.1 2.7 fusion.31
  676.8 2.4 reshape.493
  681.3 7.7 pad_maximum_fusion
  689.7 19.4 %pmax.7 = f32[3]{0:T(128)S(1)} all-reduce(f32[3]{0:T(128)S(1)} %broadcast_maximum_fusion), channel_id=1, replica_groups=mesh['shard'=2,'ctx'=4,'tp'=4] {'shard','ctx'}, use_global_device_ids=true, to_apply=%region_32.33 | all-reduce | flops 3 | bytes 24 | tf_op jit(solution)/shard_map/pmax | solution.py:239
  710.0 22.3 %reduce-scatter.16.cloned.1.call-done = f32[96,6]{1,0:T(8,128)} async-done(((f32[768,6]{1,0:T(8,128)}), f32[96,6]{1,0:T(8,128)}) %reduce-scatter.16.cloned.1.call-update) | async-done | bytes 2320
  734.6 63.3 %reduce-scatter.18.cloned.1.call-done = f32[144,1]{1,0:T(8,128)} async-done(((f32[1152,1]{1,0:T(8,128)}), f32[144,1]{1,0:T(8,128)}) %reduce-scatter.18.cloned.1.call-update) | async-done | bytes 592
  800.1 42.6 %all-reduce.13.cloned.1.call-done = bf16[1024,768]{1,0:T(8,128)(2,1)} async-done(((bf16[1024,768]{1,0:T(8,128)(2,1)}), bf16[1024,768]{1,0:T(8,128)(2,1)}) %all-reduce.13.cloned.1.call-update) | async-done | bytes 1572880 | tf_op jit(solution)/shard_map/psum | solution.py:302
  842.7 3.9 fusion.26
  846.7 162.3 %reduce-scatter.14.cloned.1.call-done = f32[24,96,96]{2,1,0:T(8,128)} async-done(((f32[192,96,96]{2,1,0:T(8,128)}), f32[24,96,96]{2,1,0:T(8,128)}) %reduce-scatter.14.cloned.1.call-update) | async-done | bytes 884752 | tf_op jit(solution)/shard_map/reduce_scatter | solution.py:312
  1008.9 2.5 fusion.72
  1011.5 2.4 fusion.35
  1013.9 3.2 fusion.36
  1017.0 3.6 fusion.37
  (285 shorter events, 71.4 us)
Async XLA Ops:
  7.2 1001.7 %copy-start = (f32[24,96,96]{2,1,0:T(8,128)S(1)}, f32[24,96,96]{2,1,0:T(8,128)}, u32[]{:S(2)}) copy-start(f32[24,96,96]{2,1,0:T(8,128)} %param.21) | copy-start | bytes 2654212
  7.2 85.6 %all-gather.6.cloned.1.call-start = ((), (), s32[]{:S(2)}) async-start(), calls=%async_computation.5 | async-start | bytes 5308416 | tf_op jit(solution)/shard_map/all_gather | solution.py:165
  9.5 127.0 %all-gather.10.cloned.1.call-start = ((), (), s32[]{:S(2)}) async-start(), calls=%async_computation.14 | async-start | bytes 1966080 | tf_op jit(solution)/shard_map/all_gather | solution.py:187
  95.8 5.2 copy-start.65
  95.8 5.2 copy-start.64
  100.1 3.5 copy-start.73
  100.9 6.9 slice-start.1
  101.0 73.7 %all-gather.8.cloned.1.call-start = ((), (), s32[]{:S(2)}) async-start(), calls=%async_computation.13 | async-start | bytes 1966080 | tf_op jit(solution)/shard_map/all_gather | solution.py:188
  103.4 186.4 %all-reduce.7.cloned.1.call-start = ((), (), s32[]{:S(2)}) async-start(), calls=%async_computation.6 | async-start | bytes 6291456 | tf_op jit(solution)/shard_map/psum | solution.py:225
  196.4 12.3 %copy-start.12 = (bf16[16,64,3,64]{1,0,3,2:T(8,128)(2,1)S(1)}, bf16[16,64,3,64]{1,0,3,2:T(8,128)(2,1)}, u32[]{:S(2)}) copy-start(bf16[16,64,3,64]{1,0,3,2:T(8,128)(2,1)} %reshape_squeeze_reshape.7) | copy-start | bytes 1179652
  208.7 3.3 copy-start.21
  211.9 3.7 copy-start.1
  212.0 3.7 copy-start.37
  212.0 4.2 copy-start.7
  216.2 3.8 copy-start.32
  220.0 3.2 copy-start.52
  222.3 147.8 %all-reduce.9.cloned.1.call-start = ((), (), s32[]{:S(2)}) async-start(), calls=%async_computation.7 | async-start | bytes 6291456 | tf_op jit(solution)/shard_map/psum | solution.py:234
  223.9 68.9 %copy-start.43 = (f32[768]{0:T(1024)}, f32[768]{0:T(1024)S(1)}, u32[]{:S(2)}) copy-start(f32[768]{0:T(1024)S(1)} %get-tuple-element.22) | copy-start | bytes 9220
  223.9 68.9 %copy-start.49 = (f32[768]{0:T(1024)}, f32[768]{0:T(1024)S(1)}, u32[]{:S(2)}) copy-start(f32[768]{0:T(1024)S(1)} %get-tuple-element.21) | copy-start | bytes 9220
  233.3 56.5 %copy-start.23 = (bf16[1,1024,768]{2,1,0:T(8,128)(2,1)S(1)}, bf16[1,1024,768]{2,1,0:T(8,128)(2,1)}, u32[]{:S(2)}) copy-start(bf16[1,1024,768]{2,1,0:T(8,128)(2,1)} %param.12) | copy-start | bytes 4718596
  294.6 3.1 copy-start.31
  294.6 3.1 copy-start.69
  301.5 160.0 %all-reduce.11.cloned.1.call-start = ((), (), s32[]{:S(2)}) async-start(), calls=%async_computation.8 | async-start | bytes 6291456 | tf_op jit(solution)/shard_map/psum | solution.py:257
  374.6 3.1 copy-start.55
  380.6 7.9 copy-start.5
  380.6 3.6 copy-start.76
  380.6 7.9 copy-start.45
  381.5 7.0 copy-start.26
  392.8 68.7 %copy-start.42 = (f32[1024]{0:T(1024)S(1)}, f32[1024]{0:T(1024)}, u32[]{:S(2)}) copy-start(f32[1024]{0:T(1024)} %copy-done.41) | copy-start | bytes 12292
  392.8 68.7 %copy-start.44 = (f32[768]{0:T(1024)S(1)}, f32[768]{0:T(1024)}, u32[]{:S(2)}) copy-start(f32[768]{0:T(1024)} %copy-done.43) | copy-start | bytes 9220
  392.8 68.7 %copy-start.46 = (f32[1024]{0:T(1024)S(1)}, f32[1024]{0:T(1024)}, u32[]{:S(2)}) copy-start(f32[1024]{0:T(1024)} %copy-done.45) | copy-start | bytes 12292
  392.8 269.5 %reduce-scatter.12.cloned.1.call-start = ((), (), s32[]{:S(2)}) async-start(), calls=%async_computation.10 | async-start | bytes 1966080 | tf_op jit(solution)/shard_map/reduce_scatter | solution.py:291
  393.6 73.3 %copy-start.51 = (f32[1024]{0:T(1024)S(1)}, f32[1024]{0:T(1024)}, u32[]{:S(2)}) copy-start(f32[1024]{0:T(1024)} %copy-done.50) | copy-start | bytes 12292
  461.5 5.4 copy-start.3
  468.4 3.8 copy-start.33
  473.4 7.2 copy-start.11
  548.4 119.6 %reduce-scatter.10.cloned.1.call-start = ((), (), s32[]{:S(2)}) async-start(), calls=%async_computation.9 | async-start | bytes 1966080 | tf_op jit(solution)/shard_map/reduce_scatter | solution.py:288
  555.4 5.5 copy-start.13
  629.6 3.1 copy-start.71
  632.4 99.9 %reduce-scatter.16.cloned.1.call-start = ((), (), s32[]{:S(2)}) async-start(), calls=%async_computation.15 | async-start | bytes 442368
  639.5 4.3 copy-start.25
  639.5 4.3 copy-start.78
  645.3 6.9 copy-start.56
  647.8 4.9 copy-start.60
  647.8 5.5 copy-start.59
  647.8 6.0 copy-start.9
  647.8 6.0 copy-start.10
  655.7 3.7 copy-start.16
  655.7 5.4 copy-start.57
  655.7 5.4 copy-start.54
  655.7 5.4 copy-start.53
  659.4 4.0 copy-start.67
  659.4 4.0 copy-start.68
  659.4 8.6 copy-start.36
  662.2 135.6 %reduce-scatter.18.cloned.1.call-start = ((), (), s32[]{:S(2)}) async-start(), calls=%async_computation.16 | async-start | bytes 663552
  664.6 178.1 %all-reduce.13.cloned.1.call-start = ((), (), s32[]{:S(2)}) async-start(), calls=%async_computation.11 | async-start | bytes 3145728 | tf_op jit(solution)/shard_map/psum | solution.py:302
  668.0 4.5 copy-start.17
  668.0 4.5 copy-start.20
  672.1 336.8 %reduce-scatter.14.cloned.1.call-start = ((), (), s32[]{:S(2)}) async-start(), calls=%async_computation.12 | async-start | bytes 10616832 | tf_op jit(solution)/shard_map/reduce_scatter | solution.py:312
  733.2 109.5 %copy-start.58 = (f32[6,96]{1,0:T(8,128)}, f32[6,96]{1,0:T(8,128)S(1)}, u32[]{:S(2)}) copy-start(f32[6,96]{1,0:T(8,128)S(1)} %copy.138) | copy-start | bytes 6916
  798.8 43.9 %copy-start.66 = (f32[1,144]{1,0:T(1,128)}, f32[1,144]{1,0:T(1,128)S(1)}, u32[]{:S(2)}) copy-start(f32[1,144]{1,0:T(1,128)S(1)} %copy.140) | copy-start | bytes 1732
  846.7 164.8 %copy-start.18 = (f32[24,96,96]{2,1,0:T(8,128)S(1)}, f32[24,96,96]{2,1,0:T(8,128)}, u32[]{:S(2)}) copy-start(f32[24,96,96]{2,1,0:T(8,128)} %param.16) | copy-start | bytes 2654212
  846.7 164.8 %copy-start.27 = (f32[24,96,96]{2,1,0:T(8,128)S(1)}, f32[24,96,96]{2,1,0:T(8,128)}, u32[]{:S(2)}) copy-start(f32[24,96,96]{2,1,0:T(8,128)} %param.22) | copy-start | bytes 2654212
  1013.9 3.2 copy-start.29
  (29 other events, 42.9 us)
Sparse Core Ops, SparseCore 0:
  10.7 82.0 all-gather.5
  101.1 35.3 all-gather.9
  138.7 35.9 all-gather.7
  222.5 67.2 all-reduce.6
  301.6 68.5 all-reduce.8
  392.9 68.5 all-reduce.10
  548.5 35.4 reduce-scatter.11
  632.5 35.4 reduce-scatter.9
  671.3 61.0 reduce-scatter.15
  736.0 61.7 reduce-scatter.17
  800.8 41.8 all-reduce.12
  846.7 162.1 reduce-scatter.13
where the time goes:
time: 1030 us
  waiting for transfers between devices  597 us (58%)
  local copies, waits for them, and re-layouts  215 us (21%)
  other arithmetic  108 us (10%)
  matrix products  69.6 us (7%)
  blocking collectives  19.4 us (2%)
  between operations  16.1 us (2%)
    reduce_scatter x1, waiting for transfers between devices, per_device(): lax.psum_scatter(blocks_grad, ('shard', 'ctx'), scatter_dimension=0, tile...  162 us
    unnamed x14, waiting for transfers between devices  85.7 us
    all_gather x1, waiting for transfers between devices, per_device(): lax.all_gather(master_blocks.astype(jnp.bfloat16), ('shard', 'ctx'), axis...  83.2 us
    psum x1, waiting for transfers between devices, per_device(): lax.psum(jnp.dot(d_gate_low, wb_up.T, preferred_element_type=jnp.float32)...  67.9 us
    psum x1, waiting for transfers between devices, per_device(): lax.psum(jnp.dot(act_low, w_down, preferred_element_type=jnp.float32), 'tp')  67.8 us
    reshape x4, local copies, waits for them, and re-layouts, pick_blocks(): picked.reshape(clipped.shape[0], clipped.shape[1] * BLOCK, head_count, HEAD)  56.3 us
    psum x1, waiting for transfers between devices, per_device(): lax.psum(jnp.dot(attended_low, w_out, preferred_element_type=jnp.float32)...  52.6 us
    psum x1, waiting for transfers between devices, per_device(): lax.psum(jnp.dot(d_proj, wb_qkv.T, preferred_element_type=jnp.float32).as...  42.6 us
  transfers between devices with their start and end apart: 12, of which 11 were waited for; matrix products, arithmetic and copies ran while one was open for 19% of the time, Pallas kernels for 0%

commit v1 on v0

--- a/solution.py
+++ b/solution.py
@@ -16,6 +16,27 @@
 rate_vector = 0.001
 neg_large = -1e30
 high = lax.Precision.HIGHEST
+
+
+def deliver_streams_in(u, lane_axis):
+    heard = lax.axis_size(lane_axis)
+    earlier, val2, latest = (heard, lax.axis_index(lane_axis), u.shape[0])
+    vec_out, odd = (u, 1)
+    while odd < earlier:
+        vec_out = jnp.concatenate(
+            [
+                vec_out,
+                lax.ppermute(
+                    vec_out,
+                    axis_name=lane_axis,
+                    perm=[(ii, (ii - odd) % earlier) for ii in range(earlier)],
+                ),
+            ],
+            0,
+        )
+        odd = 2 * odd
+    block_out = jnp.roll(vec_out, val2 * latest, 0)
+    return block_out
 
 
 def layer_norm(values, gain, shift):
@@ -162,9 +183,7 @@
     block_count = SEQ // BLOCK
     ctx_index = lax.axis_index("ctx")
     owner_index = lax.axis_index(("shard", "ctx"))
-    gathered = lax.all_gather(
-        master_blocks.astype(jnp.bfloat16), ("shard", "ctx"), axis=0, tiled=True
-    )
+    gathered = deliver_streams_in(master_blocks.astype(jnp.bfloat16), ("shard", "ctx"))
     w_qkv, w_out, w_up, w_down = unpack_weights(gathered, head_cols, unit_count)
     flat_in = inputs.reshape(-1, D)
     inner_row = inner_biases[0]

time: 1030 us -> 1090 us (1.058)
  local copies, waits for them, and re-layouts: 215 us -> 244 us
  waiting for transfers between devices: 597 us -> 613 us
    ppermute x0 -> x3, waiting for transfers between devices: none -> 114 us  [deliver_streams_in(): lax.ppermute(vec_out, axis_name=lane_axis, perm=[(ii, (ii - odd) % earlie...]
    all_gather x1, waiting for transfers between devices: 83.2 us -> 1.37 us  [per_device(): lax.all_gather(master_blocks.astype(jnp.bfloat16), ('shard', 'ctx'), axis...]
    psum x1, waiting for transfers between devices: 67.8 us -> 54.6 us  [per_device(): lax.psum(jnp.dot(act_low, w_down, preferred_element_type=jnp.float32), 'tp')]
    unnamed x164 -> x124, local copies, waits for them, and re-layouts: 19.5 us -> 27.9 us
  transfers between devices with their start and end apart: 12 -> 15, of which waited for: 11 -> 14; matrix products, arithmetic and copies ran while one was open for 19% -> 21% of each run, Pallas kernels for 0% -> 0%
where the time goes in v1:
time: 1090 us; the launch traced here: 1080 us
  waiting for transfers between devices  613 us (56%)
  local copies, waits for them, and re-layouts  244 us (22%)
  other arithmetic  110 us (10%)
  matrix products  69.1 us (6%)
  blocking collectives  21.1 us (2%)
  between operations  17 us (2%)
    reduce_scatter x1, waiting for transfers between devices, per_device(): lax.psum_scatter(blocks_grad, ('shard', 'ctx'), scatter_dimension=0, tile...  162 us
    ppermute x3, waiting for transfers between devices, deliver_streams_in(): lax.ppermute(vec_out, axis_name=lane_axis, perm=[(ii, (ii - odd) % earlie...  114 us
    unnamed x14, waiting for transfers between devices  85.4 us
    psum x1, waiting for transfers between devices, per_device(): lax.psum(jnp.dot(d_gate_low, wb_up.T, preferred_element_type=jnp.float32)...  67.2 us
    reshape x4, local copies, waits for them, and re-layouts, pick_blocks(): picked.reshape(clipped.shape[0], clipped.shape[1] * BLOCK, head_count, HEAD)  56.3 us
    psum x1, waiting for transfers between devices, per_device(): lax.psum(jnp.dot(attended_low, w_out, preferred_element_type=jnp.float32)...  56 us
    psum x1, waiting for transfers between devices, per_device(): lax.psum(jnp.dot(act_low, w_down, preferred_element_type=jnp.float32), 'tp')  54.6 us
    psum x1, waiting for transfers between devices, per_device(): lax.psum(jnp.dot(d_proj, wb_qkv.T, preferred_element_type=jnp.float32).as...  42.4 us
  transfers between devices with their start and end apart: 15, of which 14 were waited for; matrix products, arithmetic and copies ran while one was open for 21% of the time, Pallas kernels for 0%

profile of v1, /device:TPU:0, one launch (start us, length us, event | category | flops | bytes accessed | tf_op | source)
XLA Modules:
  0.0 1084.3 jit_solution(11033030616503704753)
XLA Ops:
  10.4 6.0 collective-permute-start
  16.4 12.6 %collective-permute-done = bf16[24,96,96]{2,1,0:T(8,128)(2,1)S(1)} collective-permute-done((bf16[24,96,96]{2,1,0:T(8,128)(2,1)S(1)}, bf16[24,96,96]{2,1,0:T(8,128)(2,1)S(1)}, u32[]{:S(2)}, u32[]{:S(2)}) %collective-permute-start) | collective-permute-done | bytes 442400 | tf_op jit(solution)/shard_map/ppermute | solution.py:29
  30.8 51.6 %collective-permute-done.1 = bf16[48,96,96]{2,1,0:T(8,128)(2,1)S(1)} collective-permute-done((bf16[48,96,96]{2,1,0:T(8,128)(2,1)S(1)}, bf16[48,96,96]{2,1,0:T(8,128)(2,1)S(1)}, u32[]{:S(2)}, u32[]{:S(2)}) %collective-permute-start.1) | collective-permute-done | bytes 884768 | tf_op jit(solution)/shard_map/ppermute | solution.py:29
  86.8 49.4 %collective-permute-done.2 = bf16[96,96,96]{2,1,0:T(8,128)(2,1)} collective-permute-done((bf16[96,96,96]{2,1,0:T(8,128)(2,1)}, bf16[96,96,96]{2,1,0:T(8,128)(2,1)}, u32[]{:S(2)}, u32[]{:S(2)}) %collective-permute-start.2) | collective-permute-done | bytes 1769504 | tf_op jit(solution)/shard_map/ppermute | solution.py:29
  136.2 3.2 constant_dynamic-update-slice_fusion.4
  142.3 3.3 constant_dynamic-update-slice_fusion
  149.6 2.8 convolution_bitcast_fusion
  166.9 25.1 %all-gather.10.cloned.1.call-done = bf16[4096,192]{0,1:T(8,128)(2,1)} async-done(((bf16[1024,192]{0,1:T(8,128)(2,1)}), bf16[4096,192]{0,1:T(8,128)(2,1)}) %all-gather.10.cloned.1.call-update) | async-done | bytes 1572880 | tf_op jit(solution)/shard_map/all_gather | solution.py:206
  192.0 3.1 copy.111
  195.1 2.8 gather_fusion.1
  198.0 15.9 %reshape.583 = bf16[16,512,3,64]{3,2,1,0:T(4,128)(2,1)} reshape(bf16[128,64,192]{2,1,0:T(8,128)(2,1)} %gather_fusion.1) | data formatting | bytes 6291456 | tf_op jit(solution)/shard_map/reshape | solution.py:94
  213.9 12.2 %copy.114 = bf16[16,512,3,64]{1,3,2,0:T(8,128)(2,1)} copy(bf16[16,512,3,64]{3,2,1,0:T(4,128)(2,1)} %reshape.583) | data formatting | bytes 6291456 | tf_op jit(solution)/shard_map/reshape | solution.py:94
  226.1 4.0 all-gather.8.cloned.1.call-done
  230.1 3.1 copy.106
  233.2 2.8 gather_fusion
  236.1 15.9 %reshape.582 = bf16[16,512,3,64]{3,2,1,0:T(4,128)(2,1)} reshape(bf16[128,64,192]{2,1,0:T(8,128)(2,1)} %gather_fusion) | data formatting | bytes 6291456 | tf_op jit(solution)/shard_map/reshape | solution.py:94
  251.9 12.3 %copy.115 = bf16[16,512,3,64]{1,3,2,0:T(8,128)(2,1)} copy(bf16[16,512,3,64]{3,2,1,0:T(4,128)(2,1)} %reshape.582) | data formatting | bytes 6291456 | tf_op jit(solution)/shard_map/reshape | solution.py:94
  264.2 3.2 fusion.24
  267.5 3.6 select_reduce_fusion
  271.6 2.7 fusion.38
  279.0 3.2 constant_dynamic-slice_fusion
  289.2 56.0 %all-reduce.7.cloned.1.call-done = f32[1024,768]{1,0:T(8,128)} async-done(((f32[1024,768]{1,0:T(8,128)}), f32[1024,768]{1,0:T(8,128)}) %all-reduce.7.cloned.1.call-update) | async-done | bytes 3145744 | tf_op jit(solution)/shard_map/psum | solution.py:244
  345.2 2.8 fusion.65
  353.5 3.8 fusion.60
  362.7 3.9 reshape.508
  368.4 3.0 reshape.510
  371.3 54.6 %all-reduce.9.cloned.1.call-done = f32[1024,768]{1,0:T(8,128)} async-done(((f32[1024,768]{1,0:T(8,128)}), f32[1024,768]{1,0:T(8,128)}) %all-reduce.9.cloned.1.call-update) | async-done | bytes 3145744 | tf_op jit(solution)/shard_map/psum | solution.py:253
  426.0 3.8 fusion.64
  433.5 2.8 fusion.63
  440.2 4.3 convert_reduce_fusion
  445.7 3.1 fusion.70
  450.3 67.2 %all-reduce.11.cloned.1.call-done = f32[1024,768]{1,0:T(8,128)} async-done(((f32[1024,768]{1,0:T(8,128)}), f32[1024,768]{1,0:T(8,128)}) %all-reduce.11.cloned.1.call-update) | async-done | bytes 3145744 | tf_op jit(solution)/shard_map/psum | solution.py:276
  517.6 4.7 multiply_reduce_fusion.1
  528.8 7.2 fusion.20
  536.0 15.1 %copy.148 = f32[16,512,3,64]{3,2,1,0:T(4,128)} copy(f32[16,512,3,64]{1,3,2,0:T(8,128)} %fusion.20) | data formatting | bytes 12582912 | tf_op jit(solution)/shard_map/reshape | solution.py:153
  551.1 18.9 %reshape.577 = f32[128,64,192]{2,1,0:T(8,128)} reshape(f32[16,512,3,64]{3,2,1,0:T(4,128)} %copy.148) | data formatting | bytes 12582912 | tf_op jit(solution)/shard_map/reshape | solution.py:153
  572.4 26.1 %scatter_fusion.1 = f32[64,64,192]{2,1,0:T(8,128)} fusion(f32[64,64,192]{2,1,0:T(8,128)} %broadcast.358.clone, s32[128]{0:T(128)S(1)} %reshape.532, f32[128,64,192]{2,1,0:T(8,128)} %reshape.577), kind=kCustom, calls=%fused_computation.3 | custom fusion | flops 1572864 | bytes 18874880 | tf_op jit(solution)/shard_map/scatter-add | solution.py:153
  598.4 2.5 convert_element_type.178
  600.9 2.7 copy.134
  603.7 6.7 multiply_reduce_fusion
  610.5 3.9 multiply_convert_fusion
  616.1 3.6 multiply_bitcast_fusion
  619.7 15.1 %copy.147 = f32[16,512,3,64]{3,2,1,0:T(4,128)} copy(f32[16,512,3,64]{1,3,2,0:T(8,128)} %multiply_bitcast_fusion) | data formatting | bytes 12582912 | tf_op jit(solution)/shard_map/reshape | solution.py:148
  634.8 18.9 %reshape.576 = f32[128,64,192]{2,1,0:T(8,128)} reshape(f32[16,512,3,64]{3,2,1,0:T(4,128)} %copy.147) | data formatting | bytes 12582912 | tf_op jit(solution)/shard_map/reshape | solution.py:148
  656.2 26.2 %scatter_fusion = f32[64,64,192]{2,1,0:T(8,128)} fusion(f32[64,64,192]{2,1,0:T(8,128)} %broadcast.358.clone.1, s32[128]{0:T(128)S(1)} %reshape.532, f32[128,64,192]{2,1,0:T(8,128)} %reshape.576), kind=kCustom, calls=%fused_computation.2 | custom fusion | flops 1572864 | bytes 18874880 | tf_op jit(solution)/shard_map/scatter-add | solution.py:148
  682.4 2.5 convert_element_type.174
  684.9 2.8 copy.130
  691.6 3.3 fusion.72
  695.0 2.6 reshape.520
  697.5 4.2 copy.138
  703.7 2.6 reshape.522
  706.3 4.3 copy.139
  723.7 4.1 convolution_convert_fusion
  729.7 2.7 fusion.30
  736.9 7.7 pad_maximum_fusion
  745.2 21.1 %pmax.7 = f32[3]{0:T(128)S(1)} all-reduce(f32[3]{0:T(128)S(1)} %broadcast_maximum_fusion), channel_id=1, replica_groups=mesh['shard'=2,'ctx'=4,'tp'=4] {'shard','ctx'}, use_global_device_ids=true, to_apply=%region_32.33 | all-reduce | flops 3 | bytes 24 | tf_op jit(solution)/shard_map/pmax | solution.py:258
  767.3 21.3 %reduce-scatter.16.cloned.1.call-done = f32[96,6]{1,0:T(8,128)} async-done(((f32[768,6]{1,0:T(8,128)}), f32[96,6]{1,0:T(8,128)}) %reduce-scatter.16.cloned.1.call-update) | async-done | bytes 2320
  790.9 63.4 %reduce-scatter.18.cloned.1.call-done = f32[144,1]{1,0:T(8,128)} async-done(((f32[1152,1]{1,0:T(8,128)}), f32[144,1]{1,0:T(8,128)}) %reduce-scatter.18.cloned.1.call-update) | async-done | bytes 592
  856.5 42.4 %all-reduce.13.cloned.1.call-done = bf16[1024,768]{1,0:T(8,128)(2,1)} async-done(((bf16[1024,768]{1,0:T(8,128)(2,1)}), bf16[1024,768]{1,0:T(8,128)(2,1)}) %all-reduce.13.cloned.1.call-update) | async-done | bytes 1572880 | tf_op jit(solution)/shard_map/psum | solution.py:321
  899.0 3.9 fusion.26
  902.9 162.4 %reduce-scatter.14.cloned.1.call-done = f32[24,96,96]{2,1,0:T(8,128)} async-done(((f32[192,96,96]{2,1,0:T(8,128)}), f32[24,96,96]{2,1,0:T(8,128)}) %reduce-scatter.14.cloned.1.call-update) | async-done | bytes 884752 | tf_op jit(solution)/shard_map/reduce_scatter | solution.py:331
  1065.3 2.5 fusion.73
  1070.2 3.2 fusion.35
  1073.4 3.6 fusion.36
  (265 shorter events, 110.7 us)
Async XLA Ops:
  8.0 1057.3 %copy-start = (f32[24,96,96]{2,1,0:T(8,128)S(1)}, f32[24,96,96]{2,1,0:T(8,128)}, u32[]{:S(2)}) copy-start(f32[24,96,96]{2,1,0:T(8,128)} %param.21) | copy-start | bytes 2654212
  8.0 184.0 %all-gather.10.cloned.1.call-start = ((), (), s32[]{:S(2)}) async-start(), calls=%async_computation.14 | async-start | bytes 1966080 | tf_op jit(solution)/shard_map/all_gather | solution.py:206
  10.4 129.1 %copy-start.7 = (bf16[24,96,96]{2,1,0:T(8,128)(2,1)}, bf16[24,96,96]{2,1,0:T(8,128)(2,1)S(1)}, u32[]{:S(2)}) copy-start(bf16[24,96,96]{2,1,0:T(8,128)(2,1)S(1)} %get-tuple-element.41) | copy-start | bytes 1327108
  10.4 18.6 %collective-permute-start = (bf16[24,96,96]{2,1,0:T(8,128)(2,1)S(1)}, bf16[24,96,96]{2,1,0:T(8,128)(2,1)S(1)}, u32[]{:S(2)}, u32[]{:S(2)}) collective-permute-start(bf16[24,96,96]{2,1,0:T(8,128)(2,1)S(1)} %get-tuple-element.41), channel_id=1, source_target_pairs={{0,28},{4,0},{8,4},{12,8},{16,12},{20,16},{24,20},{28,24},{1,29},{... | collective-permute-start | bytes 1327112 | tf_op jit(solution)/shard_map/ppermute | solution.py:29
  29.2 53.1 %collective-permute-start.1 = (bf16[48,96,96]{2,1,0:T(8,128)(2,1)S(1)}, bf16[48,96,96]{2,1,0:T(8,128)(2,1)S(1)}, u32[]{:S(2)}, u32[]{:S(2)}) collective-permute-start(bf16[48,96,96]{2,1,0:T(8,128)(2,1)S(1)} %pad_maximum_fusion.2), channel_id=1, source_target_pairs={{0,24},{4,28},{8,0},{12,4},{16,8},{20,12},{24,16},{28,20},{1,25},{... | collective-permute-start | bytes 2654216 | tf_op jit(solution)/shard_map/ppermute | solution.py:29
  84.3 51.9 %collective-permute-start.2 = (bf16[96,96,96]{2,1,0:T(8,128)(2,1)}, bf16[96,96,96]{2,1,0:T(8,128)(2,1)}, u32[]{:S(2)}, u32[]{:S(2)}) collective-permute-start(bf16[96,96,96]{2,1,0:T(8,128)(2,1)} %pad_maximum_fusion.1), channel_id=1, source_target_pairs={{0,16},{4,20},{8,24},{12,28},{16,0},{20,4},{24,8},{28,12},{1,17},{... | collective-permute-start | bytes 5308424 | tf_op jit(solution)/shard_map/ppermute | solution.py:29
  149.6 3.7 copy-start.44
  149.6 4.2 copy-start.43
  153.3 76.8 %all-gather.8.cloned.1.call-start = ((), (), s32[]{:S(2)}) async-start(), calls=%async_computation.13 | async-start | bytes 1966080 | tf_op jit(solution)/shard_map/all_gather | solution.py:207
  155.0 190.2 %all-reduce.7.cloned.1.call-start = ((), (), s32[]{:S(2)}) async-start(), calls=%async_computation.5 | async-start | bytes 6291456 | tf_op jit(solution)/shard_map/psum | solution.py:244
  251.9 12.3 %copy-start.13 = (bf16[16,64,3,64]{1,0,3,2:T(8,128)(2,1)S(1)}, bf16[16,64,3,64]{1,0,3,2:T(8,128)(2,1)}, u32[]{:S(2)}) copy-start(bf16[16,64,3,64]{1,0,3,2:T(8,128)(2,1)} %reshape_squeeze_reshape.7) | copy-start | bytes 1179652
  264.2 3.3 copy-start.22
  267.5 3.7 copy-start.1
  267.5 4.2 copy-start.8
  271.6 3.8 copy-start.32
  275.4 2.3 copy-start.20
  275.5 3.5 copy-start.35
  277.8 81.1 %all-gather.6.cloned.1.call-start = ((), (), s32[]{:S(2)}) async-start(), calls=%async_computation.7 | async-start | bytes 5308416 | tf_op jit(solution)/shard_map/all_gather | solution.py:262
  278.3 147.6 %all-reduce.9.cloned.1.call-start = ((), (), s32[]{:S(2)}) async-start(), calls=%async_computation.6 | async-start | bytes 6291456 | tf_op jit(solution)/shard_map/psum | solution.py:253
  278.9 157.7 %copy-start.48 = (f32[768]{0:T(1024)}, f32[768]{0:T(1024)S(1)}, u32[]{:S(2)}) copy-start(f32[768]{0:T(1024)S(1)} %slice_reduce_fusion.3) | copy-start | bytes 9220
  348.0 1.7 copy-start.2
  348.5 1.9 copy-start.30
  350.4 3.0 copy-start.31
  357.3 160.3 %all-reduce.11.cloned.1.call-start = ((), (), s32[]{:S(2)}) async-start(), calls=%async_computation.8 | async-start | bytes 6291456 | tf_op jit(solution)/shard_map/psum | solution.py:276
  436.3 8.2 copy-start.5
  436.3 2.1 copy-start.29
  436.3 3.9 copy-start.53
  436.6 7.9 copy-start.24
  448.9 271.8 %reduce-scatter.12.cloned.1.call-start = ((), (), s32[]{:S(2)}) async-start(), calls=%async_computation.10 | async-start | bytes 1966080 | tf_op jit(solution)/shard_map/reduce_scatter | solution.py:310
  517.6 4.8 copy-start.3
  523.8 1.7 copy-start.6
  528.8 7.3 copy-start.12
  603.7 120.0 %reduce-scatter.10.cloned.1.call-start = ((), (), s32[]{:S(2)}) async-start(), calls=%async_computation.9 | async-start | bytes 1966080 | tf_op jit(solution)/shard_map/reduce_scatter | solution.py:307
  610.4 5.6 copy-start.14
  614.4 1.7 copy-start.9
  687.7 100.9 %reduce-scatter.16.cloned.1.call-start = ((), (), s32[]{:S(2)}) async-start(), calls=%async_computation.15 | async-start | bytes 442368
  697.5 4.2 copy-start.25
  697.5 4.2 copy-start.49
  697.5 4.2 copy-start.54
  706.3 4.9 copy-start.39
  706.3 5.4 copy-start.38
  706.3 6.0 copy-start.10
  706.3 6.0 copy-start.11
  714.2 3.7 copy-start.17
  714.2 5.4 copy-start.36
  717.9 1.7 copy-start.40
  717.9 1.7 copy-start.41
  717.9 1.7 copy-start.42
  717.9 4.0 copy-start.46
  717.9 4.0 copy-start.47
  717.9 5.8 copy-start.34
  720.6 133.6 %reduce-scatter.18.cloned.1.call-start = ((), (), s32[]{:S(2)}) async-start(), calls=%async_computation.16 | async-start | bytes 663552
  723.0 175.9 %all-reduce.13.cloned.1.call-start = ((), (), s32[]{:S(2)}) async-start(), calls=%async_computation.11 | async-start | bytes 3145728 | tf_op jit(solution)/shard_map/psum | solution.py:321
  723.7 4.4 copy-start.18
  723.7 4.4 copy-start.21
  727.8 1.9 copy-start.33
  727.8 337.5 %reduce-scatter.14.cloned.1.call-start = ((), (), s32[]{:S(2)}) async-start(), calls=%async_computation.12 | async-start | bytes 10616832 | tf_op jit(solution)/shard_map/reduce_scatter | solution.py:331
  789.5 109.5 %copy-start.37 = (f32[6,96]{1,0:T(8,128)}, f32[6,96]{1,0:T(8,128)S(1)}, u32[]{:S(2)}) copy-start(f32[6,96]{1,0:T(8,128)S(1)} %copy.150) | copy-start | bytes 6916
  855.2 43.8 %copy-start.45 = (f32[1,144]{1,0:T(1,128)}, f32[1,144]{1,0:T(1,128)S(1)}, u32[]{:S(2)}) copy-start(f32[1,144]{1,0:T(1,128)S(1)} %copy.152) | copy-start | bytes 1732
  902.9 164.9 %copy-start.19 = (f32[24,96,96]{2,1,0:T(8,128)S(1)}, f32[24,96,96]{2,1,0:T(8,128)}, u32[]{:S(2)}) copy-start(f32[24,96,96]{2,1,0:T(8,128)} %param.16) | copy-start | bytes 2654212
  902.9 164.9 %copy-start.26 = (f32[24,96,96]{2,1,0:T(8,128)S(1)}, f32[24,96,96]{2,1,0:T(8,128)}, u32[]{:S(2)}) copy-start(f32[24,96,96]{2,1,0:T(8,128)} %param.22) | copy-start | bytes 2654212
  1067.8 2.4 copy-start.4
  1067.8 2.4 copy-start.27
  1070.2 3.2 copy-start.28
  (9 other events, 10.2 us)
Sparse Core Ops, SparseCore 0:
  153.4 38.5 all-gather.9
  194.1 35.9 all-gather.7
  277.9 67.2 all-reduce.6
  357.4 68.5 all-reduce.8
  449.0 68.5 all-reduce.10
  603.8 35.7 reduce-scatter.11
  687.8 35.7 reduce-scatter.9
  727.5 61.0 reduce-scatter.15
  792.5 61.7 reduce-scatter.17
  857.0 41.8 all-reduce.12
  903.1 162.1 reduce-scatter.13
Sparse Core Ops, SparseCore 1:
  280.9 77.9 all-gather.5
